TPU v7x, 32 devices: a whole 2x2x4 slice. The times are simulated.
32 devices in a mesh: group: 1, expert: 16 (over z, y, x), step: 2 (over core).
Axes of the slice: x: 2, y: 2, z: 4, core: 2. Of those that a mesh axis runs over, the one named last changes fastest.
Arguments:
- latents: float32 [2, 2048, 1536], P('step', ('group', 'expert')), may hold values from -6 to 6
- modulation: float32 [2, 6, 1536], P('group'), may hold values from -3 to 3
- shallow_routes: int32 [2, 2048, 2], P('step', ('group', 'expert')), may hold values from 0 to 3, all different within a row; in each aligned block of 128 rows (0 to 127, 128 to 255, ..., all dimensions but the last counted through in order) at most 64 rows name the same one
- deep_routes: int32 [2048, 2], P(('group', 'expert')), may hold values from 0 to 3, all different within a row; in each aligned block of 128 rows (0 to 127, 128 to 255, ...) at most 64 rows name the same one
- refresh: int32 [16], P(('group', 'expert')), may hold values from 0 to 1
- shallow_in: bfloat16 [16, 1536, 768], P('expert'), may hold values from -0.15625 to 0.15625
- shallow_out: bfloat16 [16, 768, 1536], P('expert'), may hold values from -0.109375 to 0.109375
- deep_in: bfloat16 [16, 1536, 768], P('expert'), may hold values from -0.15625 to 0.15625
- deep_out: bfloat16 [16, 768, 1536], P('expert'), may hold values from -0.109375 to 0.109375
- shallow_router: float32 [1536, 4], replicated, may hold values from -0.15625 to 0.15625
- deep_router: float32 [1536, 4], replicated, may hold values from -0.15625 to 0.15625
Outputs:
- result: bfloat16 [2, 2048, 1536], P('step', ('group', 'expert'))
Inputs may be any that keep to these rules, and one draw needn't show every extreme that they name: `shallow_routes`: within the 128 rows of one index of expert (aligned blocks), each expert is named by at most 64 rows, and by exactly 64 rows in some block; a row names two different experts. `deep_routes`: within the 128 rows of one index of expert (aligned blocks), each expert is named by at most 64 rows, and by exactly 64 rows in some block; a row names two different experts.
All inputs are finite; a program needn't handle non-finite values.
Results may differ from a plain program's by a relative error of at most 0.01.
Values may be sent and summed in bfloat16 or wider, within the bound.
No kernel may reach another device: no remote copies, remote signals or barrier semaphores. Data moves between devices by JAX's collectives and lax.ppermute only.
A program may use at most 64 MiB of HBM per device.

v0:
```python
import jax
import jax.numpy as jnp
from jax import lax
from jax.sharding import PartitionSpec as P


def from_root(block, axis, owner):
    block = jnp.where(lax.axis_index(axis) == owner, block, jnp.zeros_like(block))
    return lax.psum(block, axis)


def modulate(hidden, shift_row, scale_row):
    average = jnp.mean(hidden, axis=-1, keepdims=True)
    centred = hidden - average
    variance = jnp.mean(centred * centred, axis=-1, keepdims=True)
    return (centred * lax.rsqrt(variance + 1e-06) * (1.0 + scale_row) + shift_row).astype(
        jnp.bfloat16
    )


def plan(normed, routes, router, capacity):
    rows_count, width = normed.shape
    experts = router.shape[1]
    logits = jnp.dot(normed.astype(jnp.float32), router, precision=lax.Precision.HIGHEST)
    hits = routes[:, :, None] == jnp.arange(experts, dtype=jnp.int32)
    chosen = jnp.sum(jnp.where(hits, logits[:, None, :], 0.0), axis=-1)
    gate_sig = jax.nn.sigmoid(chosen)
    weights = gate_sig / jnp.sum(gate_sig, axis=-1, keepdims=True)
    pair_hits = hits.reshape(rows_count * 2, experts).astype(jnp.int32)
    position = jnp.sum(pair_hits * (jnp.cumsum(pair_hits, axis=0) - 1), axis=-1).reshape(
        rows_count, 2
    )
    slot_hit = position[:, :, None] == jnp.arange(capacity, dtype=jnp.int32)
    placed = hits[:, :, :, None] & slot_hit[:, :, None, :]
    dispatch = jnp.any(placed, axis=1).reshape(rows_count, experts * capacity).astype(jnp.bfloat16)
    gathered = jnp.einsum("rs,rd->sd", dispatch, normed, preferred_element_type=jnp.float32).astype(
        jnp.bfloat16
    )
    combine_w = jnp.sum(jnp.where(placed, weights[:, :, None, None], 0.0), axis=1)
    return (gathered.reshape(experts, capacity, width), combine_w)


def spread(gathered, slices):
    experts, capacity, width = gathered.shape
    quarters = slices // experts
    return jnp.broadcast_to(gathered[:, None], (experts, quarters, capacity, width)).reshape(
        slices, capacity, width
    )


def expert_rows(piece, weight_in, weight_out):
    dims = piece.shape
    flat_rows = piece.reshape(-1, dims[-1])
    hidden = jax.nn.gelu(
        jnp.dot(flat_rows, weight_in, preferred_element_type=jnp.float32), approximate=True
    ).astype(jnp.bfloat16)
    return (
        jnp.dot(hidden, weight_out, preferred_element_type=jnp.float32)
        .astype(jnp.bfloat16)
        .reshape(dims)
    )


def combine(summed, combine_w):
    rows_count = combine_w.shape[0]
    width = summed.shape[-1]
    return jnp.dot(
        combine_w.reshape(rows_count, -1),
        summed.reshape(-1, width),
        precision=lax.Precision.HIGHEST,
        preferred_element_type=jnp.float32,
    )


def finish(returned, combine_w):
    experts = combine_w.shape[1]
    width = returned.shape[2]
    summed = jnp.sum(
        returned.astype(jnp.float32).reshape(experts, -1, returned.shape[1], width), axis=1
    )
    return combine(summed, combine_w)


def body(
    latents,
    modulation,
    shallow_routes,
    deep_routes,
    refresh,
    shallow_in,
    shallow_out,
    deep_in,
    deep_out,
    shallow_router,
    deep_router,
):
    slices = lax.axis_size("expert")
    experts = shallow_router.shape[1]
    rows_count = latents.shape[1]
    capacity = 2 * max(rows_count * 5 // 64, rows_count // experts)
    step_idx = lax.axis_index("step")
    root_idx = refresh[0]
    own_mod = lax.dynamic_index_in_dim(modulation, step_idx, 0, keepdims=False)
    features = latents[0]
    normed = modulate(features, own_mod[0], own_mod[1])
    gathered, combine_w = plan(normed, shallow_routes[0], shallow_router, capacity)
    partial_value = expert_rows(
        lax.all_to_all(spread(gathered, slices), "expert", split_axis=0, concat_axis=0, tiled=True),
        shallow_in[0],
        shallow_out[0],
    )
    returned = lax.all_to_all(partial_value, "expert", split_axis=0, concat_axis=0, tiled=True)
    moe_shallow = finish(returned, combine_w)
    after_shallow = (features + own_mod[2] * moe_shallow).astype(jnp.bfloat16)
    normed_deep = modulate(after_shallow.astype(jnp.float32), own_mod[3], own_mod[4])
    gathered_deep, combine_deep = plan(normed_deep, deep_routes, deep_router, capacity)
    partial_value = expert_rows(
        lax.all_to_all(
            spread(gathered_deep, slices), "expert", split_axis=0, concat_axis=0, tiled=True
        ),
        deep_in[0],
        deep_out[0],
    )
    returned_deep = lax.all_to_all(partial_value, "expert", split_axis=0, concat_axis=0, tiled=True)
    moe_deep = finish(returned_deep, combine_deep)
    own_delta = (own_mod[5] * moe_deep).astype(jnp.bfloat16)
    deep_delta = from_root(own_delta, "step", root_idx)
    result = (after_shallow.astype(jnp.float32) + deep_delta.astype(jnp.float32)).astype(
        jnp.bfloat16
    )
    return result[None]


def solution(mesh):
    in_specs = (
        P("step", ("group", "expert"), None),
        P("group", None, None),
        P("step", ("group", "expert"), None),
        P(("group", "expert"), None),
        P(("group", "expert")),
        P("expert", None, None),
        P("expert", None, None),
        P("expert", None, None),
        P("expert", None, None),
        P(),
        P(),
    )
    out_specs = P("step", ("group", "expert"), None)
    return jax.shard_map(body, mesh=mesh, in_specs=in_specs, out_specs=out_specs, check_vma=False)
```

profile of v0, /device:TPU:0, one launch (start us, length us, event | category | flops | bytes accessed | tf_op | source)
XLA Modules:
  0.0 376.2 jit_solution(6678324923360058093)
XLA Ops:
  6.5 0.0 copy-start
  6.5 0.9 copy.32
  7.5 0.1 eq.123
  7.6 0.1 eq.119
  7.8 1.3 reduce_sum.127
  9.0 1.4 multiply_reduce_fusion.1
  10.4 0.7 iota_compare_fusion.5
  11.1 1.2 reduce-window.14
  12.3 0.1 slice.46
  12.4 0.1 copy.34
  12.5 0.1 copy.35
  12.6 0.1 add_bitcast_fusion.1
  12.7 0.1 eq.127
  12.9 0.1 copy.36
  13.0 0.9 dynamic-slice_reduce_fusion.1
  13.9 1.6 convolution_convert_fusion.3
  15.6 0.3 broadcast_in_dim.82
  15.9 79.5 %all_to_all.20 = bf16[16,64,1536]{2,1,0:T(8,128)(2,1)} all-to-all(bf16[16,64,1536]{2,1,0:T(8,128)(2,1)S(1)} %bitcast.112), channel_id=1, replica_groups=mesh['group'=1,'expert'=16,'step'=2] {'expert'}, dimensions={0} | all-to-all | bytes 6291456 | tf_op jit(solution)/shard_map/all_to_all | solution.py:108
  95.4 0.0 copy-done
  95.4 10.4 %convolution_convert_fusion.1 = bf16[1024,1536]{1,0:T(8,128)(2,1)} fusion(bf16[1,768,1536]{2,1,0:T(8,128)(2,1)S(1)} %copy-done, bf16[1024,1536]{1,0:T(8,128)(2,1)} %bitcast.116, bf16[1,1536,768]{2,1,0:T(8,128)(2,1)} %param.16), kind=kOutput, calls=%fused_computation.5 | convolution fusion | flops 4840488960 | bytes 11010048 | tf_op jit(solution)/shard_map/dot_general | solution.py:58
  105.8 0.0 copy-start.7
  105.8 0.0 copy-start.1
  105.8 0.0 copy-start.4
  105.8 0.0 copy-start.6
  105.8 4.6 %all-to-all-start.1 = ((bf16[16,64,1536]{2,1,0:T(8,128)(2,1)}), bf16[16,64,1536]{2,1,0:T(8,128)(2,1)}, u32[]{:S(2)}, u32[]{:S(2)}) async-start(bf16[16,64,1536]{2,1,0:T(8,128)(2,1)} %bitcast.114), calls=%async_computation.1 | async-start | bytes 6291456 | tf_op jit(solution)/shard_map/all_to_all | solution.py:112
  110.5 0.0 copy-done.7
  110.5 0.1 copy.37
  110.6 0.1 eq.139
  110.7 0.1 eq.135
  110.9 1.2 reduce-window.16
  112.1 0.1 slice.47
  112.2 0.1 copy.39
  112.3 0.1 copy.40
  112.4 0.1 add_bitcast_fusion
  112.5 0.1 eq.143
  112.7 0.1 copy.41
  112.7 0.0 copy-done.1
  112.7 0.0 copy-done.4
  112.7 0.5 fusion.44
  113.3 0.0 copy-done.6
  113.5 57.2 %all-to-all-done.1 = bf16[16,64,1536]{2,1,0:T(8,128)(2,1)} async-done(((bf16[16,64,1536]{2,1,0:T(8,128)(2,1)}), bf16[16,64,1536]{2,1,0:T(8,128)(2,1)}, u32[]{:S(2)}, u32[]{:S(2)}) %all-to-all-start.1) | async-done | bytes 3145760 | tf_op jit(solution)/shard_map/all_to_all | solution.py:112
  170.7 2.6 convert_reduce_fusion.1
  173.2 1.1 fusion.61
  174.3 0.0 copy-start.2
  174.3 0.2 multiply_reduce_fusion
  174.6 0.2 add_convert_fusion.1
  174.8 0.3 convolution_convert_fusion.2
  175.1 0.1 copy-done.2
  175.2 0.3 broadcast_in_dim.86
  175.5 84.7 %all_to_all.21 = bf16[16,64,1536]{2,1,0:T(8,128)(2,1)} all-to-all(bf16[16,64,1536]{2,1,0:T(8,128)(2,1)S(1)} %bitcast.113), channel_id=1, replica_groups=mesh['group'=1,'expert'=16,'step'=2] {'expert'}, dimensions={0} | all-to-all | bytes 6291456 | tf_op jit(solution)/shard_map/all_to_all | solution.py:118
  260.3 11.1 %convolution_convert_fusion = bf16[1024,1536]{1,0:T(8,128)(2,1)} fusion(bf16[1,768,1536]{2,1,0:T(8,128)(2,1)} %param.19, bf16[1024,1536]{1,0:T(8,128)(2,1)} %bitcast.117, bf16[1,1536,768]{2,1,0:T(8,128)(2,1)} %param.18), kind=kOutput, calls=%fused_computation.4 | convolution fusion | flops 4840488960 | bytes 11010048 | tf_op jit(solution)/shard_map/dot_general | solution.py:58
  271.4 4.6 %all-to-all-start.3 = ((bf16[16,64,1536]{2,1,0:T(8,128)(2,1)}), bf16[16,64,1536]{2,1,0:T(8,128)(2,1)}, u32[]{:S(2)}, u32[]{:S(2)}) async-start(bf16[16,64,1536]{2,1,0:T(8,128)(2,1)} %bitcast.115), calls=%async_computation.3 | async-start | bytes 6291456 | tf_op jit(solution)/shard_map/all_to_all | solution.py:124
  276.0 0.0 all-reduce.2.cloned.1.call-start
  276.7 0.0 copy-done.5
  276.7 0.4 fusion.62
  277.2 0.1 fusion.46
  277.3 0.0 copy-start.3
  277.3 58.9 %all-to-all-done.3 = bf16[16,64,1536]{2,1,0:T(8,128)(2,1)} async-done(((bf16[16,64,1536]{2,1,0:T(8,128)(2,1)}), bf16[16,64,1536]{2,1,0:T(8,128)(2,1)}, u32[]{:S(2)}, u32[]{:S(2)}) %all-to-all-start.3) | async-done | bytes 3145760 | tf_op jit(solution)/shard_map/all_to_all | solution.py:124
  336.2 2.6 convert_reduce_fusion
  338.7 1.7 fusion.22
  340.5 0.0 all-reduce.2.cloned.1.call-update
  340.5 27.0 %all-reduce.2.cloned.1.call-done = bf16[128,1536]{1,0:T(8,128)(2,1)} async-done(((bf16[128,1536]{1,0:T(8,128)(2,1)}), bf16[128,1536]{1,0:T(8,128)(2,1)}) %all-reduce.2.cloned.1.call-update) | async-done | bytes 393232 | tf_op jit(solution)/shard_map/psum | solution.py:9
  367.6 0.0 copy-done.3
  367.6 1.8 fusion.39
  (25 shorter events, 0.5 us)
Async XLA Ops:
  6.5 88.8 %copy-start = (bf16[1,768,1536]{2,1,0:T(8,128)(2,1)S(1)}, bf16[1,768,1536]{2,1,0:T(8,128)(2,1)}, u32[]{:S(2)}) copy-start(bf16[1,768,1536]{2,1,0:T(8,128)(2,1)} %param.17) | copy-start | bytes 7077892
  105.8 4.7 %copy-start.7 = (s32[128,2]{0,1:T(2,128)S(1)}, s32[128,2]{0,1:T(2,128)}, u32[]{:S(2)}) copy-start(s32[128,2]{0,1:T(2,128)} %param.14) | copy-start | bytes 3076
  105.8 6.9 %copy-start.1 = (f32[1,128,1536]{2,1,0:T(8,128)S(1)}, f32[1,128,1536]{2,1,0:T(8,128)}, u32[]{:S(2)}) copy-start(f32[1,128,1536]{2,1,0:T(8,128)} %param.11) | copy-start | bytes 2359300
  105.8 6.9 %copy-start.4 = (f32[1536,4]{0,1:T(4,128)S(1)}, f32[1536,4]{0,1:T(4,128)}, u32[]{:S(2)}) copy-start(f32[1536,4]{0,1:T(4,128)} %param.20) | copy-start | bytes 73732
  105.8 7.4 %copy-start.6 = (s32[1,128,2]{1,2,0:T(2,128)S(1)}, s32[1,128,2]{1,2,0:T(2,128)}, u32[]{:S(2)}) copy-start(s32[1,128,2]{1,2,0:T(2,128)} %param.13) | copy-start | bytes 3076
  105.8 64.8 %all-to-all-start.1 = ((bf16[16,64,1536]{2,1,0:T(8,128)(2,1)}), bf16[16,64,1536]{2,1,0:T(8,128)(2,1)}, u32[]{:S(2)}, u32[]{:S(2)}) async-start(bf16[16,64,1536]{2,1,0:T(8,128)(2,1)} %bitcast.114), calls=%async_computation.1 | async-start | bytes 6291456 | tf_op jit(solution)/shard_map/all_to_all | solution.py:112
  174.3 0.9 copy-start.2
  271.4 5.3 %copy-start.5 = (f32[1536,4]{0,1:T(4,128)S(1)}, f32[1536,4]{0,1:T(4,128)}, u32[]{:S(2)}) copy-start(f32[1536,4]{0,1:T(4,128)} %param.21) | copy-start | bytes 73732
  271.4 64.8 %all-to-all-start.3 = ((bf16[16,64,1536]{2,1,0:T(8,128)(2,1)}), bf16[16,64,1536]{2,1,0:T(8,128)(2,1)}, u32[]{:S(2)}, u32[]{:S(2)}) async-start(bf16[16,64,1536]{2,1,0:T(8,128)(2,1)} %bitcast.115), calls=%async_computation.3 | async-start | bytes 6291456 | tf_op jit(solution)/shard_map/all_to_all | solution.py:124
  276.0 91.6 %all-reduce.2.cloned.1.call-start = ((), (), s32[]{:S(2)}) async-start(), calls=%async_computation.4 | async-start | bytes 786432 | tf_op jit(solution)/shard_map/psum | solution.py:9
  277.3 90.3 %copy-start.3 = (f32[128,1536]{1,0:T(8,128)S(1)}, f32[128,1536]{1,0:T(8,128)}, u32[]{:S(2)}) copy-start(f32[128,1536]{1,0:T(8,128)} %copy-done.2) | copy-start | bytes 2359300
Sparse Core Ops, SparseCore 0:
  340.6 26.8 all-reduce.1
where the time goes:
time: 377 us; the launch traced here: 376 us
  blocking collectives  164 us (44%)
  waiting for transfers between devices  143 us (38%)
  matrix products  27.3 us (7%)
  other arithmetic  14.7 us (4%)
  between operations  14.3 us (4%)
  starting transfers between devices  9.3 us (2%)
    all_to_all x2, waiting for transfers between devices, body(): lax.all_to_all(partial_value, 'expert', split_axis=0, concat_axis=0, tile...  116 us
    all_to_all x1, blocking collectives, body(): lax.all_to_all(spread(gathered_deep, slices), 'expert', split_axis=0, con...  84.7 us
    all_to_all x1, blocking collectives, body(): lax.all_to_all(spread(gathered, slices), 'expert', split_axis=0, concat_a...  79.5 us
    psum x1, waiting for transfers between devices, from_root(): return lax.psum(block, axis)  27 us
    dot_general x2, matrix products, expert_rows(): jnp.dot(hidden, weight_out, preferred_element_type=jnp.float32)  21.5 us
    all_to_all x2, starting transfers between devices, body(): lax.all_to_all(partial_value, 'expert', split_axis=0, concat_axis=0, tile...  9.25 us
  transfers between devices with their start and end apart: 3, of which 3 were waited for; matrix products, arithmetic and copies ran while one was open for 1% of the time, Pallas kernels for 0%

commit v1 on v0

--- a/solution.py
+++ b/solution.py
@@ -4,9 +4,15 @@
 from jax.sharding import PartitionSpec as P
 
 
+def add_all(x, mesh_axis):
+    pieces = lax.all_gather(x, mesh_axis, axis=0, tiled=False)
+    summed = pieces.sum(axis=0)
+    return summed
+
+
 def from_root(block, axis, owner):
     block = jnp.where(lax.axis_index(axis) == owner, block, jnp.zeros_like(block))
-    return lax.psum(block, axis)
+    return add_all(block, axis)
 
 
 def modulate(hidden, shift_row, scale_row):

time: 377 us -> 347 us (0.920)
  the two profiles are of different devices: /device:TPU:0 before, /device:TPU:13 now
where the time goes in v1:
time: 347 us; the launch traced here: 346 us
  blocking collectives  154 us (44%)
  waiting for transfers between devices  137 us (39%)
  matrix products  26.5 us (8%)
  other arithmetic  15 us (4%)
  starting transfers between devices  10.1 us (3%)
    all_to_all x2, waiting for transfers between devices, body(): lax.all_to_all(partial_value, 'expert', split_axis=0, concat_axis=0, tile...  137 us
    all_to_all x1, blocking collectives, body(): lax.all_to_all(spread(gathered, slices), 'expert', split_axis=0, concat_a...  76.2 us
    all_to_all x1, blocking collectives, body(): lax.all_to_all(spread(gathered_deep, slices), 'expert', split_axis=0, con...  73.9 us
    dot_general x2, matrix products, expert_rows(): jnp.dot(hidden, weight_out, preferred_element_type=jnp.float32)  21.5 us
    all_to_all x2, starting transfers between devices, body(): lax.all_to_all(partial_value, 'expert', split_axis=0, concat_axis=0, tile...  10.1 us
  transfers between devices with their start and end apart: 2, of which 2 were waited for; matrix products, arithmetic and copies ran while one was open for 1% of the time, Pallas kernels for 0%

profile of v1, /device:TPU:13, one launch (start us, length us, event | category | flops | bytes accessed | tf_op | source)
XLA Modules:
  0.0 346.2 jit_solution(7170594384440726311)
XLA Ops:
  0.0 0.0 copy-start
  0.0 0.9 copy.32
  0.9 0.1 eq.123
  1.1 0.1 eq.119
  1.2 1.3 reduce_sum.139
  2.5 1.4 multiply_reduce_fusion.1
  3.9 0.7 iota_compare_fusion.5
  4.6 1.2 reduce-window.14
  5.8 0.1 slice.46
  5.9 0.1 copy.34
  6.0 0.1 copy.35
  6.1 0.1 add_bitcast_fusion.1
  6.2 0.1 eq.127
  6.3 0.1 copy.36
  6.5 0.9 dynamic-slice_reduce_fusion.1
  7.4 1.6 convolution_convert_fusion.3
  9.0 0.3 broadcast_in_dim.82
  9.3 76.2 %all_to_all.20 = bf16[16,64,1536]{2,1,0:T(8,128)(2,1)} all-to-all(bf16[16,64,1536]{2,1,0:T(8,128)(2,1)S(1)} %bitcast.113), channel_id=1, replica_groups=mesh['group'=1,'expert'=16,'step'=2] {'expert'}, dimensions={0} | all-to-all | bytes 6291456 | tf_op jit(solution)/shard_map/all_to_all | solution.py:114
  85.5 0.0 copy-done
  85.5 10.4 %convolution_convert_fusion.1 = bf16[1024,1536]{1,0:T(8,128)(2,1)} fusion(bf16[1,768,1536]{2,1,0:T(8,128)(2,1)S(1)} %copy-done, bf16[1024,1536]{1,0:T(8,128)(2,1)} %bitcast.117, bf16[1,1536,768]{2,1,0:T(8,128)(2,1)} %param.16), kind=kOutput, calls=%fused_computation.5 | convolution fusion | flops 4840488960 | bytes 11010048 | tf_op jit(solution)/shard_map/dot_general | solution.py:64
  95.9 0.0 copy-start.7
  95.9 0.0 copy-start.1
  95.9 0.0 copy-start.4
  95.9 0.0 copy-start.6
  95.9 5.0 %all-to-all-start.1 = ((bf16[16,64,1536]{2,1,0:T(8,128)(2,1)}), bf16[16,64,1536]{2,1,0:T(8,128)(2,1)}, u32[]{:S(2)}, u32[]{:S(2)}) async-start(bf16[16,64,1536]{2,1,0:T(8,128)(2,1)} %bitcast.115), calls=%async_computation.1 | async-start | bytes 6291456 | tf_op jit(solution)/shard_map/all_to_all | solution.py:118
  100.9 0.0 copy-done.7
  100.9 0.1 copy.37
  101.0 0.1 eq.139
  101.2 0.1 eq.135
  101.3 1.2 reduce-window.16
  102.6 0.1 slice.47
  102.6 0.1 copy.39
  102.8 0.1 copy.40
  102.9 0.1 add_bitcast_fusion
  103.0 0.1 eq.143
  103.1 0.1 copy.41
  103.2 0.0 copy-done.1
  103.2 0.0 copy-done.4
  103.2 0.5 fusion.44
  103.7 0.0 copy-done.6
  103.9 67.6 %all-to-all-done.1 = bf16[16,64,1536]{2,1,0:T(8,128)(2,1)} async-done(((bf16[16,64,1536]{2,1,0:T(8,128)(2,1)}), bf16[16,64,1536]{2,1,0:T(8,128)(2,1)}, u32[]{:S(2)}, u32[]{:S(2)}) %all-to-all-start.1) | async-done | bytes 3145760 | tf_op jit(solution)/shard_map/all_to_all | solution.py:118
  171.5 2.6 convert_reduce_fusion.1
  174.1 1.1 fusion.61
  175.2 0.0 copy-start.2
  175.2 0.2 multiply_reduce_fusion
  175.4 0.2 add_convert_fusion.1
  175.6 0.3 convolution_convert_fusion.2
  176.0 0.1 copy-done.2
  176.1 0.3 broadcast_in_dim.86
  176.4 73.9 %all_to_all.21 = bf16[16,64,1536]{2,1,0:T(8,128)(2,1)} all-to-all(bf16[16,64,1536]{2,1,0:T(8,128)(2,1)S(1)} %bitcast.114), channel_id=1, replica_groups=mesh['group'=1,'expert'=16,'step'=2] {'expert'}, dimensions={0} | all-to-all | bytes 6291456 | tf_op jit(solution)/shard_map/all_to_all | solution.py:124
  250.2 11.1 %convolution_convert_fusion = bf16[1024,1536]{1,0:T(8,128)(2,1)} fusion(bf16[1,768,1536]{2,1,0:T(8,128)(2,1)} %param.19, bf16[1024,1536]{1,0:T(8,128)(2,1)} %bitcast.118, bf16[1,1536,768]{2,1,0:T(8,128)(2,1)} %param.18), kind=kOutput, calls=%fused_computation.4 | convolution fusion | flops 4840488960 | bytes 11010048 | tf_op jit(solution)/shard_map/dot_general | solution.py:64
  261.4 0.0 copy-start.5
  261.4 5.1 %all-to-all-start.3 = ((bf16[16,64,1536]{2,1,0:T(8,128)(2,1)}), bf16[16,64,1536]{2,1,0:T(8,128)(2,1)}, u32[]{:S(2)}, u32[]{:S(2)}) async-start(bf16[16,64,1536]{2,1,0:T(8,128)(2,1)} %bitcast.116), calls=%async_computation.3 | async-start | bytes 6291456 | tf_op jit(solution)/shard_map/all_to_all | solution.py:130
  267.1 0.0 copy-done.5
  267.1 0.4 fusion.62
  267.6 0.1 fusion.46
  267.6 69.4 %all-to-all-done.3 = bf16[16,64,1536]{2,1,0:T(8,128)(2,1)} async-done(((bf16[16,64,1536]{2,1,0:T(8,128)(2,1)}), bf16[16,64,1536]{2,1,0:T(8,128)(2,1)}, u32[]{:S(2)}, u32[]{:S(2)}) %all-to-all-start.3) | async-done | bytes 3145760 | tf_op jit(solution)/shard_map/all_to_all | solution.py:130
  337.0 2.6 convert_reduce_fusion
  339.6 0.0 copy-start.3
  339.6 1.0 fusion.22
  340.6 3.5 %all-gather = bf16[256,1536]{1,0:T(8,128)(2,1)} all-gather(bf16[128,1536]{1,0:T(8,128)(2,1)S(1)} %fusion.22), channel_id=2, replica_groups=mesh['group'=1,'expert'=16,'step'=2] {'step'}, dimensions={0}, use_global_device_ids=true | all-gather | bytes 1179648 | tf_op jit(solution)/shard_map/all_gather | solution.py:8
  344.1 1.3 reduce_sum.152
  345.4 0.0 copy-done.3
  345.4 0.8 fusion.39
  (24 shorter events, 0.5 us)
Async XLA Ops:
  0.0 85.5 %copy-start = (bf16[1,768,1536]{2,1,0:T(8,128)(2,1)S(1)}, bf16[1,768,1536]{2,1,0:T(8,128)(2,1)}, u32[]{:S(2)}) copy-start(bf16[1,768,1536]{2,1,0:T(8,128)(2,1)} %param.17) | copy-start | bytes 7077892
  95.9 5.0 %copy-start.7 = (s32[128,2]{0,1:T(2,128)S(1)}, s32[128,2]{0,1:T(2,128)}, u32[]{:S(2)}) copy-start(s32[128,2]{0,1:T(2,128)} %param.14) | copy-start | bytes 3076
  95.9 7.3 %copy-start.1 = (f32[1,128,1536]{2,1,0:T(8,128)S(1)}, f32[1,128,1536]{2,1,0:T(8,128)}, u32[]{:S(2)}) copy-start(f32[1,128,1536]{2,1,0:T(8,128)} %param.11) | copy-start | bytes 2359300
  95.9 7.3 %copy-start.4 = (f32[1536,4]{0,1:T(4,128)S(1)}, f32[1536,4]{0,1:T(4,128)}, u32[]{:S(2)}) copy-start(f32[1536,4]{0,1:T(4,128)} %param.20) | copy-start | bytes 73732
  95.9 7.8 %copy-start.6 = (s32[1,128,2]{1,2,0:T(2,128)S(1)}, s32[1,128,2]{1,2,0:T(2,128)}, u32[]{:S(2)}) copy-start(s32[1,128,2]{1,2,0:T(2,128)} %param.13) | copy-start | bytes 3076
  95.9 75.6 %all-to-all-start.1 = ((bf16[16,64,1536]{2,1,0:T(8,128)(2,1)}), bf16[16,64,1536]{2,1,0:T(8,128)(2,1)}, u32[]{:S(2)}, u32[]{:S(2)}) async-start(bf16[16,64,1536]{2,1,0:T(8,128)(2,1)} %bitcast.115), calls=%async_computation.1 | async-start | bytes 6291456 | tf_op jit(solution)/shard_map/all_to_all | solution.py:118
  175.2 0.9 copy-start.2
  261.4 5.7 %copy-start.5 = (f32[1536,4]{0,1:T(4,128)S(1)}, f32[1536,4]{0,1:T(4,128)}, u32[]{:S(2)}) copy-start(f32[1536,4]{0,1:T(4,128)} %param.21) | copy-start | bytes 73732
  261.4 75.7 %all-to-all-start.3 = ((bf16[16,64,1536]{2,1,0:T(8,128)(2,1)}), bf16[16,64,1536]{2,1,0:T(8,128)(2,1)}, u32[]{:S(2)}, u32[]{:S(2)}) async-start(bf16[16,64,1536]{2,1,0:T(8,128)(2,1)} %bitcast.116), calls=%async_computation.3 | async-start | bytes 6291456 | tf_op jit(solution)/shard_map/all_to_all | solution.py:130
  339.6 5.8 %copy-start.3 = (f32[128,1536]{1,0:T(8,128)S(1)}, f32[128,1536]{1,0:T(8,128)}, u32[]{:S(2)}) copy-start(f32[128,1536]{1,0:T(8,128)} %copy-done.2) | copy-start | bytes 2359300
